TPU v7x, 128 devices: a whole 4x4x4 slice. The times are simulated.
128 devices in a mesh: batch: 4 (over z), head: 2 (over core), seq: 16 (over x, y).
Axes of the slice: x: 4, y: 4, z: 4, core: 2. Of those that a mesh axis runs over, the one named last changes fastest.
Arguments:
- hidden: float32 [32768, 8192], P(('batch', 'seq')), parts along dimension 0, may hold values from -6 to 6
- row_scale: float32 [32768], P(('batch', 'seq')), parts along dimension 0, may hold values from 0.25 to 4
- key_value_weight: float32 [8192, 8, 256], P('seq', 'head'), may hold values from -0.0625 to 0.0625
- outlier: int32 [512, 8], P(('batch', 'seq'), 'head'), parts along dimension 0, may hold values 0 or 1
- sketch_sign_flags: int32 [8, 2, 128, 64], P('head'), may hold values from 0 to 1
Outputs:
- left: bfloat16 [8, 32768, 128], P('head', ('batch', 'seq')), parts along dimension 1
- right: float32 [32, 128, 128], P(('batch', 'head')), parts along dimension 0
There are 4 independent parts, one for each index of `batch`. A program takes and returns all parts, laid end to end along the dimension named above; an argument that names none is the same for every part. Nothing has to cross between parts.
All inputs are finite; a program needn't handle non-finite values. No bound on the sum of `outlier` on one device may be relied on, other than what follows from the above.
Results may differ from a plain program's by a relative error of at most 0.0015.
Values sent between devices are 32-bit elements; how exact they have to be, the bound alone decides.
No kernel may reach another device: no remote copies, remote signals or barrier semaphores. Data moves between devices by JAX's collectives and lax.ppermute only.
A program may use at most 192 MiB of HBM per device.

v0:
```python
import math
import jax
import jax.numpy as jnp
from jax import lax
from jax.sharding import PartitionSpec as P

ITERS = 2
complete_cycle = 2.0 * math.pi


def shards(hidden, row_scale, key_value_weight, outlier, sketch_sign_flags):
    tok_rows = hidden.shape[0]
    head_count = key_value_weight.shape[1]
    kv_cols = key_value_weight.shape[2]
    head_dim = kv_cols // 2
    rank_cols = sketch_sign_flags.shape[3]
    group_count = outlier.shape[0]
    highest = lax.Precision.HIGHEST
    weight_piece = lax.all_gather(key_value_weight, "seq", axis=0, tiled=True)
    flat_piece = weight_piece.reshape(weight_piece.shape[0], head_count * kv_cols)
    projected_key_value = jnp.dot(hidden, flat_piece, precision=highest)
    projected_key_value = projected_key_value * row_scale[:, None]
    grouped_rows = projected_key_value.reshape(
        group_count, tok_rows // group_count, head_count, kv_cols
    )
    quantization_spacing = jnp.max(jnp.abs(grouped_rows), axis=1, keepdims=True) / 7.0 + 1e-06
    retain_mask = (1 - outlier).astype(jnp.float32)[:, None, :, None]
    residual_error = (
        retain_mask * jnp.sin(complete_cycle * grouped_rows / quantization_spacing)
    ).reshape(tok_rows, head_count, 2, head_dim)
    sign_matrix = (2 * sketch_sign_flags - 1).astype(jnp.float32)
    sketch = jnp.einsum("thec,heck->thek", residual_error, sign_matrix, precision=highest)
    for iteration in range(ITERS):
        local_gram = jnp.einsum("thek,theq->hekq", sketch, sketch, precision=highest)
        gram_matrix = lax.psum(local_gram, "seq")
        lower_factor = jnp.linalg.cholesky(gram_matrix)
        identity = jnp.broadcast_to(jnp.eye(rank_cols, dtype=gram_matrix.dtype), gram_matrix.shape)
        inverse_factor = jax.scipy.linalg.solve_triangular(lower_factor, identity, lower=True)
        basis_matrix = jnp.einsum("thek,heqk->theq", sketch, inverse_factor, precision=highest)
        local_coef = jnp.einsum("thec,theq->hecq", residual_error, basis_matrix, precision=highest)
        coefficient_rows = lax.psum(local_coef, "seq")
        if iteration + 1 < ITERS:
            sketch = jnp.einsum(
                "thec,hecq->theq", residual_error, coefficient_rows, precision=highest
            )
    root_length = math.sqrt(tok_rows * lax.axis_size("seq"))
    left = (
        (root_length * basis_matrix)
        .transpose(1, 0, 2, 3)
        .reshape(head_count, tok_rows, 2 * rank_cols)
        .astype(jnp.bfloat16)
    )
    right = (
        (coefficient_rows / root_length)
        .transpose(0, 2, 1, 3)
        .reshape(head_count, head_dim, 2 * rank_cols)
    )
    return (left, right)


def solution(mesh):
    return jax.shard_map(
        shards,
        mesh=mesh,
        in_specs=(
            P(("batch", "seq"), None),
            P(("batch", "seq")),
            P("seq", "head", None),
            P(("batch", "seq"), "head"),
            P("head", None, None, None),
        ),
        out_specs=(P("head", ("batch", "seq"), None), P(("batch", "head"), None, None)),
        check_vma=False,
    )
```

profile of v0, /device:TPU:0, one launch (start us, length us, event | category | flops | bytes accessed | tf_op | source)
XLA Modules:
  0.0 858.8 jit_solution(14637617141155702260)
XLA Ops:
  8.1 201.4 %all-gather.2.cloned.1.call-done = f32[8192,4,256]{2,1,0:T(4,128)} async-done(((f32[512,4,256]{2,1,0:T(4,128)}), f32[8192,4,256]{2,1,0:T(4,128)}) %all-gather.2.cloned.1.call-update) | async-done | bytes 33554448 | tf_op jit(solution)/shard_map/all_gather | solution.py:19
  209.6 27.5 %copy.108 = f32[1024,8,4,256]{3,1,2,0:T(8,128)} copy(f32[1024,8,4,256]{3,2,1,0:T(4,128)} %bitcast.58) | data formatting | bytes 67108864
  237.1 60.5 %multiply_abs_fusion = (f32[512,1024]{1,0:T(8,128)}, f32[512,1024]{1,0:T(8,128)}) fusion(f32[512]{0:T(512)S(1)} %copy-done.3, f32[512,8192]{1,0:T(8,128)} %param.8, f32[8192,1024]{1,0:T(8,128)} %bitcast.59), kind=kOutput, calls=%fused_computation.3 | convolution fusion | flops 51541180416 | bytes 54528000 | tf_op jit(solution)/shard_map/dot_general | solution.py:21
  297.6 2.2 abs.7
  300.3 2.1 div.32
  302.4 1.9 copy.86
  304.4 1.8 copy.88
  306.2 8.9 %fusion.1 = f32[512,4,2,128]{3,0,2,1:T(8,128)S(1)} fusion(f32[512,4,2,128]{3,0,2,1:T(8,128)} %copy.88, f32[512,4,2,128]{3,2,0,1:T(2,128)} %div.32, f32[512,4]{0,1:T(4,128)S(1)} %mul.46), kind=kLoop, calls=%fused_computation.2 | loop fusion | flops 1048576 | bytes 6299648 | tf_op jit(solution)/shard_map/mul | solution.py:29
  315.1 2.4 convolution_bitcast_fusion.1
  317.5 1.8 fusion.21
  319.4 83.9 %all-reduce.5.cloned.1.call-done = f32[4,2,64,64]{2,3,1,0:T(8,128)} async-done(((f32[4,2,64,64]{2,3,1,0:T(8,128)}), f32[4,2,64,64]{2,3,1,0:T(8,128)}) %all-reduce.5.cloned.1.call-update) | async-done | bytes 131088 | tf_op jit(solution)/shard_map/psum | solution.py:35
  404.3 1.7 fusion.9
  406.0 47.6 %custom-call.8 = f32[4,2,64,64]{3,2,1,0:T(8,128)S(1)} custom-call(f32[4,2,64,64]{3,2,1,0:T(8,128)} %fusion.9), custom_call_target="Cholesky" | custom-call | tf_op jit(solution)/shard_map/jit(cholesky)/cholesky | solution.py:36
  454.7 40.0 %custom-call.9 = f32[4,2,1,64,64]{3,4,2,1,0:T(8,128)S(1)} custom-call(f32[4,2,1,64,64]{4,3,2,1,0:T(8,128)} %select_bitcast_fusion.1), custom_call_target="InvertDiagBlocksLowerTriangular" | custom-call | tf_op jit(solution)/shard_map/jit(_solve_triangular)/vmap(vmap())/triangular_solve | solution.py:38
  496.3 2.2 fusion.22
  498.6 83.5 %all-reduce.7.cloned.1.call-done = f32[4,2,128,64]{2,3,1,0:T(8,128)} async-done(((f32[4,2,128,64]{2,3,1,0:T(8,128)}), f32[4,2,128,64]{2,3,1,0:T(8,128)}) %all-reduce.7.cloned.1.call-update) | async-done | bytes 262160 | tf_op jit(solution)/shard_map/psum | solution.py:41
  582.1 3.3 convolution_bitcast_fusion
  585.4 1.8 fusion.23
  587.3 83.6 %all-reduce.9.cloned.1.call-done = f32[4,2,64,64]{2,3,1,0:T(8,128)} async-done(((f32[4,2,64,64]{2,3,1,0:T(8,128)}), f32[4,2,64,64]{2,3,1,0:T(8,128)}) %all-reduce.9.cloned.1.call-update) | async-done | bytes 131088 | tf_op jit(solution)/shard_map/psum | solution.py:35
  673.6 47.6 %custom-call.10 = f32[4,2,64,64]{3,2,1,0:T(8,128)S(1)} custom-call(f32[4,2,64,64]{3,2,1,0:T(8,128)} %fusion.6), custom_call_target="Cholesky" | custom-call | tf_op jit(solution)/shard_map/jit(cholesky)/cholesky | solution.py:36
  722.2 40.0 %custom-call.11 = f32[4,2,1,64,64]{3,4,2,1,0:T(8,128)S(1)} custom-call(f32[4,2,1,64,64]{4,3,2,1,0:T(8,128)} %select_bitcast_fusion), custom_call_target="InvertDiagBlocksLowerTriangular" | custom-call | tf_op jit(solution)/shard_map/jit(_solve_triangular)/vmap(vmap())/triangular_solve | solution.py:38
  762.9 1.8 multiply_convert_fusion
  764.7 2.2 fusion.2
  767.9 82.5 %all-reduce.11.cloned.1.call-done = f32[4,2,128,64]{2,3,1,0:T(8,128)} async-done(((f32[4,2,128,64]{2,3,1,0:T(8,128)}), f32[4,2,128,64]{2,3,1,0:T(8,128)}) %all-reduce.11.cloned.1.call-update) | async-done | bytes 262160 | tf_op jit(solution)/shard_map/psum | solution.py:41
  (42 shorter events, 12.4 us)
Async XLA Ops:
  7.2 0.8 copy-start.2
  7.2 202.4 %all-gather.2.cloned.1.call-start = ((), (), s32[]{:S(2)}) async-start(), calls=%async_computation | async-start | bytes 35651584 | tf_op jit(solution)/shard_map/all_gather | solution.py:19
  7.9 395.4 %all-reduce.5.cloned.1.call-start = ((), (), s32[]{:S(2)}) async-start(), calls=%async_computation.1 | async-start | bytes 524288 | tf_op jit(solution)/shard_map/psum | solution.py:35
  209.6 27.5 %copy-start.3 = (f32[512]{0:T(512)S(1)}, f32[512]{0:T(512)}, u32[]{:S(2)}) copy-start(f32[512]{0:T(512)} %param.9) | copy-start | bytes 6148
  306.2 8.9 %copy-start.1 = (s32[4,2,128,64]{2,3,1,0:T(8,128)S(1)}, s32[4,2,128,64]{2,3,1,0:T(8,128)}, u32[]{:S(2)}) copy-start(s32[4,2,128,64]{2,3,1,0:T(8,128)} %param.12) | copy-start | bytes 786436
  319.3 262.8 %all-reduce.7.cloned.1.call-start = ((), (), s32[]{:S(2)}) async-start(), calls=%async_computation.2 | async-start | bytes 524288 | tf_op jit(solution)/shard_map/psum | solution.py:41
  498.6 172.3 %all-reduce.9.cloned.1.call-start = ((), (), s32[]{:S(2)}) async-start(), calls=%async_computation.3 | async-start | bytes 524288 | tf_op jit(solution)/shard_map/psum | solution.py:35
  587.2 263.2 %all-reduce.11.cloned.1.call-start = ((), (), s32[]{:S(2)}) async-start(), calls=%async_computation.4 | async-start | bytes 524288 | tf_op jit(solution)/shard_map/psum | solution.py:41
  764.7 2.3 copy-start
Sparse Core Ops, SparseCore 0:
  10.1 199.3 all-gather.1
  319.4 83.7 all-reduce.4
  498.7 83.3 all-reduce.6
  587.3 83.4 all-reduce.8
  767.1 83.3 all-reduce.10
where the time goes:
time: 860 us; the launch traced here: 859 us
  waiting for transfers between devices  536 us (62%)
  other arithmetic  191 us (22%)
  matrix products  78.2 us (9%)
  local copies, waits for them, and re-layouts  39.9 us (5%)
  between operations  14 us (2%)
    all_gather x1, waiting for transfers between devices, shards(): weight_piece = lax.all_gather(key_value_weight, 'seq', axis=0, tiled=True)  201 us
    psum x2, waiting for transfers between devices, shards(): gram_matrix = lax.psum(local_gram, 'seq')  167 us
    psum x2, waiting for transfers between devices, shards(): coefficient_rows = lax.psum(local_coef, 'seq')  166 us
    another operation x7, other arithmetic, shards(): lower_factor = jnp.linalg.cholesky(gram_matrix)  95.6 us
    another operation x5, other arithmetic, shards(): jax.scipy.linalg.solve_triangular(lower_factor, identity, lower=True)  81.7 us
    dot_general x1, matrix products, shards(): projected_key_value = jnp.dot(hidden, flat_piece, precision=highest)  60.5 us
    unnamed x11, local copies, waits for them, and re-layouts  29.4 us
  transfers between devices with their start and end apart: 5, of which 5 were waited for; matrix products, arithmetic and copies ran while one was open for 0% of the time, Pallas kernels for 0%

commit v1 on v0

--- a/solution.py
+++ b/solution.py
@@ -32,7 +32,8 @@
     sketch = jnp.einsum("thec,heck->thek", residual_error, sign_matrix, precision=highest)
     for iteration in range(ITERS):
         local_gram = jnp.einsum("thek,theq->hekq", sketch, sketch, precision=highest)
-        gram_matrix = lax.psum(local_gram, "seq")
+        blocks = lax.all_gather(local_gram, "seq", axis=0, tiled=False)
+        gram_matrix = blocks.sum(axis=0)
         lower_factor = jnp.linalg.cholesky(gram_matrix)
         identity = jnp.broadcast_to(jnp.eye(rank_cols, dtype=gram_matrix.dtype), gram_matrix.shape)
         inverse_factor = jax.scipy.linalg.solve_triangular(lower_factor, identity, lower=True)

time: 860 us -> 800 us (0.930)
  waiting for transfers between devices: 536 us -> 471 us
    psum x2 -> x0, waiting for transfers between devices: 167 us -> none  [shards(): gram_matrix = lax.psum(local_gram, 'seq')]
    all_gather x0 -> x2, waiting for transfers between devices: none -> 102 us  [shards(): blocks = lax.all_gather(local_gram, 'seq', axis=0, tiled=False)]
where the time goes in v1:
time: 800 us; the launch traced here: 799 us
  waiting for transfers between devices  471 us (59%)
  other arithmetic  196 us (24%)
  matrix products  78.2 us (10%)
  local copies, waits for them, and re-layouts  39.5 us (5%)
  between operations  14 us (2%)
    all_gather x1, waiting for transfers between devices, shards(): weight_piece = lax.all_gather(key_value_weight, 'seq', axis=0, tiled=True)  201 us
    psum x2, waiting for transfers between devices, shards(): coefficient_rows = lax.psum(local_coef, 'seq')  167 us
    all_gather x2, waiting for transfers between devices, shards(): blocks = lax.all_gather(local_gram, 'seq', axis=0, tiled=False)  102 us
    another operation x7, other arithmetic, shards(): lower_factor = jnp.linalg.cholesky(gram_matrix)  95.6 us
    another operation x5, other arithmetic, shards(): jax.scipy.linalg.solve_triangular(lower_factor, identity, lower=True)  81.7 us
    dot_general x1, matrix products, shards(): projected_key_value = jnp.dot(hidden, flat_piece, precision=highest)  60.5 us
    unnamed x11, local copies, waits for them, and re-layouts  29.4 us
  transfers between devices with their start and end apart: 5, of which 5 were waited for; matrix products, arithmetic and copies ran while one was open for 0% of the time, Pallas kernels for 0%

profile of v1, /device:TPU:0, one launch (start us, length us, event | category | flops | bytes accessed | tf_op | source)
XLA Modules:
  0.0 799.1 jit_solution(13762391619325089990)
XLA Ops:
  8.1 201.5 %all-gather.6.cloned.1.call-done = f32[8192,4,256]{2,1,0:T(4,128)} async-done(((f32[512,4,256]{2,1,0:T(4,128)}), f32[8192,4,256]{2,1,0:T(4,128)}) %all-gather.6.cloned.1.call-update) | async-done | bytes 33554448 | tf_op jit(solution)/shard_map/all_gather | solution.py:19
  209.6 27.5 %copy.92 = f32[1024,8,4,256]{3,1,2,0:T(8,128)} copy(f32[1024,8,4,256]{3,2,1,0:T(4,128)} %bitcast.60) | data formatting | bytes 67108864
  237.1 60.5 %multiply_abs_fusion = (f32[512,1024]{1,0:T(8,128)}, f32[512,1024]{1,0:T(8,128)}) fusion(f32[512]{0:T(512)S(1)} %copy-done.3, f32[512,8192]{1,0:T(8,128)} %param.8, f32[8192,1024]{1,0:T(8,128)} %bitcast.61), kind=kOutput, calls=%fused_computation.3 | convolution fusion | flops 51541180416 | bytes 54528000 | tf_op jit(solution)/shard_map/dot_general | solution.py:21
  297.6 2.2 abs.7
  300.3 2.1 div.32
  302.4 1.9 copy.74
  304.4 1.8 copy.76
  306.2 8.9 %fusion.1 = f32[512,4,2,128]{3,0,2,1:T(8,128)S(1)} fusion(f32[512,4,2,128]{3,0,2,1:T(8,128)} %copy.76, f32[512,4,2,128]{3,2,0,1:T(2,128)} %div.32, f32[512,4]{0,1:T(4,128)S(1)} %mul.46), kind=kLoop, calls=%fused_computation.2 | loop fusion | flops 1048576 | bytes 6299648 | tf_op jit(solution)/shard_map/mul | solution.py:29
  315.1 2.4 convolution_bitcast_fusion.1
  317.5 1.8 fusion.21
  319.4 51.2 %all-gather.8.cloned.1.call-done = f32[64,2,64,64]{3,2,1,0:T(8,128)} async-done(((f32[4,2,64,64]{3,2,1,0:T(8,128)}), f32[64,2,64,64]{3,2,1,0:T(8,128)}) %all-gather.8.cloned.1.call-update) | async-done | bytes 2097168 | tf_op jit(solution)/shard_map/all_gather | solution.py:35
  370.6 2.7 reduce_sum.18
  375.8 47.6 %custom-call.8 = f32[4,2,64,64]{3,2,1,0:T(8,128)S(1)} custom-call(f32[4,2,64,64]{3,2,1,0:T(8,128)} %fusion.9), custom_call_target="Cholesky" | custom-call | tf_op jit(solution)/shard_map/jit(cholesky)/cholesky | solution.py:37
  424.5 40.0 %custom-call.9 = f32[4,2,1,64,64]{3,4,2,1,0:T(8,128)S(1)} custom-call(f32[4,2,1,64,64]{4,3,2,1,0:T(8,128)} %select_bitcast_fusion.1), custom_call_target="InvertDiagBlocksLowerTriangular" | custom-call | tf_op jit(solution)/shard_map/jit(_solve_triangular)/vmap(vmap())/triangular_solve | solution.py:39
  466.1 2.2 fusion.22
  468.4 83.8 %all-reduce.3.cloned.1.call-done = f32[4,2,128,64]{2,3,1,0:T(8,128)} async-done(((f32[4,2,128,64]{2,3,1,0:T(8,128)}), f32[4,2,128,64]{2,3,1,0:T(8,128)}) %all-reduce.3.cloned.1.call-update) | async-done | bytes 262160 | tf_op jit(solution)/shard_map/psum | solution.py:42
  552.2 3.3 convolution_bitcast_fusion
  555.6 1.8 fusion.23
  557.7 50.7 %all-gather.10.cloned.1.call-done = f32[64,2,64,64]{3,2,1,0:T(8,128)} async-done(((f32[4,2,64,64]{3,2,1,0:T(8,128)}), f32[64,2,64,64]{3,2,1,0:T(8,128)}) %all-gather.10.cloned.1.call-update) | async-done | bytes 2097168 | tf_op jit(solution)/shard_map/all_gather | solution.py:35
  608.4 2.7 reduce_sum.19
  613.6 47.6 %custom-call.10 = f32[4,2,64,64]{3,2,1,0:T(8,128)S(1)} custom-call(f32[4,2,64,64]{3,2,1,0:T(8,128)} %fusion.6), custom_call_target="Cholesky" | custom-call | tf_op jit(solution)/shard_map/jit(cholesky)/cholesky | solution.py:37
  662.2 40.0 %custom-call.11 = f32[4,2,1,64,64]{3,4,2,1,0:T(8,128)S(1)} custom-call(f32[4,2,1,64,64]{4,3,2,1,0:T(8,128)} %select_bitcast_fusion), custom_call_target="InvertDiagBlocksLowerTriangular" | custom-call | tf_op jit(solution)/shard_map/jit(_solve_triangular)/vmap(vmap())/triangular_solve | solution.py:39
  704.6 2.2 fusion.2
  707.9 82.9 %all-reduce.5.cloned.1.call-done = f32[4,2,128,64]{2,3,1,0:T(8,128)} async-done(((f32[4,2,128,64]{2,3,1,0:T(8,128)}), f32[4,2,128,64]{2,3,1,0:T(8,128)}) %all-reduce.5.cloned.1.call-update) | async-done | bytes 262160 | tf_op jit(solution)/shard_map/psum | solution.py:42
  (44 shorter events, 15.6 us)
Async XLA Ops:
  7.2 0.8 copy-start.2
  7.2 202.4 %all-gather.6.cloned.1.call-start = ((), (), s32[]{:S(2)}) async-start(), calls=%async_computation | async-start | bytes 35651584 | tf_op jit(solution)/shard_map/all_gather | solution.py:19
  7.9 362.7 %all-gather.8.cloned.1.call-start = ((), (), s32[]{:S(2)}) async-start(), calls=%async_computation.3 | async-start | bytes 4456448 | tf_op jit(solution)/shard_map/all_gather | solution.py:35
  209.6 27.5 %copy-start.3 = (f32[512]{0:T(512)S(1)}, f32[512]{0:T(512)}, u32[]{:S(2)}) copy-start(f32[512]{0:T(512)} %param.9) | copy-start | bytes 6148
  306.2 8.9 %copy-start.1 = (s32[4,2,128,64]{2,3,1,0:T(8,128)S(1)}, s32[4,2,128,64]{2,3,1,0:T(8,128)}, u32[]{:S(2)}) copy-start(s32[4,2,128,64]{2,3,1,0:T(8,128)} %param.12) | copy-start | bytes 786436
  319.3 232.9 %all-reduce.3.cloned.1.call-start = ((), (), s32[]{:S(2)}) async-start(), calls=%async_computation.1 | async-start | bytes 524288 | tf_op jit(solution)/shard_map/psum | solution.py:42
  468.4 140.0 %all-gather.10.cloned.1.call-start = ((), (), s32[]{:S(2)}) async-start(), calls=%async_computation.4 | async-start | bytes 4456448 | tf_op jit(solution)/shard_map/all_gather | solution.py:35
  557.4 233.4 %all-reduce.5.cloned.1.call-start = ((), (), s32[]{:S(2)}) async-start(), calls=%async_computation.2 | async-start | bytes 524288 | tf_op jit(solution)/shard_map/psum | solution.py:42
  704.6 2.3 copy-start
Sparse Core Ops, SparseCore 0:
  10.1 199.3 all-gather.5
  319.4 51.1 all-gather.7
  468.5 83.6 all-reduce.2
  557.5 50.8 all-gather.9
  707.0 83.7 all-reduce.4

commit v2 on v0

--- a/solution.py
+++ b/solution.py
@@ -16,7 +16,10 @@
     rank_cols = sketch_sign_flags.shape[3]
     group_count = outlier.shape[0]
     highest = lax.Precision.HIGHEST
-    weight_piece = lax.all_gather(key_value_weight, "seq", axis=0, tiled=True)
+    row_out = lax.axis_size("seq")
+    current_block = jnp.stack([key_value_weight] * row_out, axis=0)
+    a_next = lax.all_to_all(current_block, "seq", split_axis=0, concat_axis=0)
+    weight_piece = jnp.concatenate(a_next, axis=0)
     flat_piece = weight_piece.reshape(weight_piece.shape[0], head_count * kv_cols)
     projected_key_value = jnp.dot(hidden, flat_piece, precision=highest)
     projected_key_value = projected_key_value * row_scale[:, None]

time: 860 us -> 1300 us (1.51)
  waiting for transfers between devices: 536 us -> 960 us
    all_to_all x0 -> x1, waiting for transfers between devices: none -> 620 us  [shards(): a_next = lax.all_to_all(current_block, 'seq', split_axis=0, concat_axis=0)]
    all_gather x1 -> x0, waiting for transfers between devices: 201 us -> none  [shards(): weight_piece = lax.all_gather(key_value_weight, 'seq', axis=0, tiled=True)]
where the time goes in v2:
time: 1300 us
  waiting for transfers between devices  960 us (74%)
  other arithmetic  191 us (15%)
  matrix products  78.2 us (6%)
  local copies, waits for them, and re-layouts  52.3 us (4%)
  between operations  14 us (1%)
    all_to_all x1, waiting for transfers between devices, shards(): a_next = lax.all_to_all(current_block, 'seq', split_axis=0, concat_axis=0)  620 us
    psum x2, waiting for transfers between devices, shards(): gram_matrix = lax.psum(local_gram, 'seq')  174 us
    psum x2, waiting for transfers between devices, shards(): coefficient_rows = lax.psum(local_coef, 'seq')  166 us
    another operation x7, other arithmetic, shards(): lower_factor = jnp.linalg.cholesky(gram_matrix)  95.6 us
    another operation x5, other arithmetic, shards(): jax.scipy.linalg.solve_triangular(lower_factor, identity, lower=True)  81.7 us
    dot_general x1, matrix products, shards(): projected_key_value = jnp.dot(hidden, flat_piece, precision=highest)  60.5 us
    unnamed x11, local copies, waits for them, and re-layouts  29.4 us
  transfers between devices with their start and end apart: 5, of which 5 were waited for; matrix products, arithmetic and copies ran while one was open for 0% of the time, Pallas kernels for 0%

profile of v2, /device:TPU:0, one launch (start us, length us, event | category | flops | bytes accessed | tf_op | source)
XLA Modules:
  0.0 1302.5 jit_solution(14148888333844979701)
XLA Ops:
  7.2 12.3 stack.2
  19.5 7.3 all-to-all-start
  27.1 620.1 %all-to-all-done = f32[16,512,4,256]{3,2,1,0:T(4,128)} async-done(((f32[16,512,4,256]{3,2,1,0:T(4,128)}), f32[16,512,4,256]{3,2,1,0:T(4,128)}, u32[]{:S(2)}, u32[]{:S(2)}) %all-to-all-start) | async-done | bytes 33554464 | tf_op jit(solution)/shard_map/all_to_all | solution.py:21
  647.1 27.5 %copy.108 = f32[1024,8,4,256]{3,1,2,0:T(8,128)} copy(f32[1024,8,4,256]{3,2,1,0:T(4,128)} %bitcast.19) | data formatting | bytes 67108864
  674.7 60.5 %multiply_abs_fusion = (f32[512,1024]{1,0:T(8,128)}, f32[512,1024]{1,0:T(8,128)}) fusion(f32[512]{0:T(512)S(1)} %copy-done.3, f32[512,8192]{1,0:T(8,128)} %param.8, f32[8192,1024]{1,0:T(8,128)} %bitcast.59), kind=kOutput, calls=%fused_computation.3 | convolution fusion | flops 51541180416 | bytes 54528000 | tf_op jit(solution)/shard_map/dot_general | solution.py:24
  735.2 2.2 abs.7
  737.8 2.1 div.32
  740.0 1.9 copy.86
  741.9 1.8 copy.88
  743.7 8.9 fusion.1
  752.6 2.4 convolution_bitcast_fusion.1
  755.0 1.8 fusion.21
  756.9 90.1 %all-reduce.5.cloned.1.call-done = f32[4,2,64,64]{2,3,1,0:T(8,128)} async-done(((f32[4,2,64,64]{2,3,1,0:T(8,128)}), f32[4,2,64,64]{2,3,1,0:T(8,128)}) %all-reduce.5.cloned.1.call-update) | async-done | bytes 131088 | tf_op jit(solution)/shard_map/psum | solution.py:38
  849.8 47.6 %custom-call.8 = f32[4,2,64,64]{3,2,1,0:T(8,128)S(1)} custom-call(f32[4,2,64,64]{3,2,1,0:T(8,128)} %fusion.9), custom_call_target="Cholesky" | custom-call | tf_op jit(solution)/shard_map/jit(cholesky)/cholesky | solution.py:39
  898.4 40.0 %custom-call.9 = f32[4,2,1,64,64]{3,4,2,1,0:T(8,128)S(1)} custom-call(f32[4,2,1,64,64]{4,3,2,1,0:T(8,128)} %select_bitcast_fusion.1), custom_call_target="InvertDiagBlocksLowerTriangular" | custom-call | tf_op jit(solution)/shard_map/jit(_solve_triangular)/vmap(vmap())/triangular_solve | solution.py:41
  940.1 2.2 fusion.22
  942.4 83.5 %all-reduce.7.cloned.1.call-done = f32[4,2,128,64]{2,3,1,0:T(8,128)} async-done(((f32[4,2,128,64]{2,3,1,0:T(8,128)}), f32[4,2,128,64]{2,3,1,0:T(8,128)}) %all-reduce.7.cloned.1.call-update) | async-done | bytes 262160 | tf_op jit(solution)/shard_map/psum | solution.py:44
  1025.8 3.3 convolution_bitcast_fusion
  1031.0 83.5 %all-reduce.9.cloned.1.call-done = f32[4,2,64,64]{2,3,1,0:T(8,128)} async-done(((f32[4,2,64,64]{2,3,1,0:T(8,128)}), f32[4,2,64,64]{2,3,1,0:T(8,128)}) %all-reduce.9.cloned.1.call-update) | async-done | bytes 131088 | tf_op jit(solution)/shard_map/psum | solution.py:38
  1117.3 47.6 %custom-call.10 = f32[4,2,64,64]{3,2,1,0:T(8,128)S(1)} custom-call(f32[4,2,64,64]{3,2,1,0:T(8,128)} %fusion.6), custom_call_target="Cholesky" | custom-call | tf_op jit(solution)/shard_map/jit(cholesky)/cholesky | solution.py:39
  1165.9 40.0 %custom-call.11 = f32[4,2,1,64,64]{3,4,2,1,0:T(8,128)S(1)} custom-call(f32[4,2,1,64,64]{4,3,2,1,0:T(8,128)} %select_bitcast_fusion), custom_call_target="InvertDiagBlocksLowerTriangular" | custom-call | tf_op jit(solution)/shard_map/jit(_solve_triangular)/vmap(vmap())/triangular_solve | solution.py:41
  1206.6 1.8 multiply_convert_fusion
  1208.4 2.2 fusion.2
  1211.6 82.5 %all-reduce.11.cloned.1.call-done = f32[4,2,128,64]{2,3,1,0:T(8,128)} async-done(((f32[4,2,128,64]{2,3,1,0:T(8,128)}), f32[4,2,128,64]{2,3,1,0:T(8,128)}) %all-reduce.11.cloned.1.call-update) | async-done | bytes 262160 | tf_op jit(solution)/shard_map/psum | solution.py:44
  (42 shorter events, 15.2 us)
Async XLA Ops:
  19.5 7.4 copy-start.2
  19.5 627.6 %all-to-all-start = ((f32[16,512,4,256]{3,2,1,0:T(4,128)}), f32[16,512,4,256]{3,2,1,0:T(4,128)}, u32[]{:S(2)}, u32[]{:S(2)}) async-start(f32[16,512,4,256]{3,2,1,0:T(4,128)} %stack.2), calls=%async_computation | async-start | bytes 67108864 | tf_op jit(solution)/shard_map/all_to_all | solution.py:21
  26.8 820.2 %all-reduce.5.cloned.1.call-start = ((), (), s32[]{:S(2)}) async-start(), calls=%async_computation.1 | async-start | bytes 524288 | tf_op jit(solution)/shard_map/psum | solution.py:38
  647.1 27.5 %copy-start.3 = (f32[512]{0:T(512)S(1)}, f32[512]{0:T(512)}, u32[]{:S(2)}) copy-start(f32[512]{0:T(512)} %param.9) | copy-start | bytes 6148
  743.7 8.9 copy-start.1
  756.8 269.0 %all-reduce.7.cloned.1.call-start = ((), (), s32[]{:S(2)}) async-start(), calls=%async_computation.2 | async-start | bytes 524288 | tf_op jit(solution)/shard_map/psum | solution.py:44
  942.3 172.2 %all-reduce.9.cloned.1.call-start = ((), (), s32[]{:S(2)}) async-start(), calls=%async_computation.3 | async-start | bytes 524288 | tf_op jit(solution)/shard_map/psum | solution.py:38
  1031.0 263.2 %all-reduce.11.cloned.1.call-start = ((), (), s32[]{:S(2)}) async-start(), calls=%async_computation.4 | async-start | bytes 524288 | tf_op jit(solution)/shard_map/psum | solution.py:44
  1208.4 2.3 copy-start
Sparse Core Ops, SparseCore 0:
  757.0 90.0 all-reduce.4
  942.4 83.3 all-reduce.6
  1031.1 83.3 all-reduce.8
  1210.7 83.3 all-reduce.10
